TPU v7x, 32 devices: a whole 2x2x4 slice. The times are simulated.
32 devices in a mesh: seq: 8 (over z, x), doc: 4 (over y, core).
Axes of the slice: x: 2, y: 2, z: 4, core: 2. Of those that a mesh axis runs over, the one named last changes fastest.
Arguments:
- queries: bfloat16 [16384, 4096], P(('doc', 'seq')), parts along dimension 0, may hold values from -24 to 24
- keys: bfloat16 [16384, 4096], P(('doc', 'seq')), parts along dimension 0, may hold values from -24 to 24
- values: bfloat16 [16384, 4096], P(('doc', 'seq')), parts along dimension 0, may hold values from -6 to 6
Outputs:
- attended: bfloat16 [16384, 4096], P(('doc', 'seq')), parts along dimension 0
There are 4 independent parts, one for each index of `doc`. A program takes and returns all parts, laid end to end along the dimension named above; each array names one. Nothing has to cross between parts.
All inputs are finite; a program needn't handle non-finite values. Where the computation divides by a largest or mean magnitude, that divisor is 1e-20 or more.
Results may differ from a plain program's by a relative error of at most 0.04.
Values may be sent and summed in bfloat16 or wider, within the bound.
A program may use at most 192 MiB of HBM per device.

v0:
```python
import jax
import jax.numpy as jnp
from jax import lax
from jax.sharding import PartitionSpec as P

H = 32
DH = 128
M = 512
ITERS = 6
D = 4096


def softmax_last(scores):
    top = jnp.max(scores, -1, keepdims=True)
    exponent_values = jnp.exp(scores - top)
    return exponent_values / jnp.sum(exponent_values, -1, keepdims=True)


def newton_schulz(kernel):
    precise = lax.Precision.HIGHEST
    row_most = jnp.max(jnp.sum(jnp.abs(kernel), 2), 1)
    col_most = jnp.max(jnp.sum(jnp.abs(kernel), 1), 1)
    inverse = jnp.swapaxes(kernel, 1, 2) / (row_most * col_most)[:, None, None]
    identity = jnp.eye(kernel.shape[1], dtype=jnp.float32)[None]
    for sweep in range(ITERS):
        kernel_inv = jnp.einsum("hij,hjk->hik", kernel, inverse, precision=precise)
        inner = jnp.einsum(
            "hij,hjk->hik", kernel_inv, 7.0 * identity - kernel_inv, precision=precise
        )
        middle = jnp.einsum("hij,hjk->hik", kernel_inv, 15.0 * identity - inner, precision=precise)
        inverse = 0.25 * jnp.einsum(
            "hij,hjk->hik", inverse, 13.0 * identity - middle, precision=precise
        )
    return inverse


def body(queries, keys, values):
    devices = lax.axis_size("seq")
    position = lax.axis_index("seq")
    tokens_here = queries.shape[0]
    per_device = M // devices
    segment = tokens_here // per_device
    owned = H // devices
    score_scale = DH ** (-0.5)
    local_q = (
        jnp.sum(queries.reshape(per_device, segment, D), axis=1, dtype=jnp.float32) / segment
    ).astype(jnp.bfloat16)
    local_k = (
        jnp.sum(keys.reshape(per_device, segment, D), axis=1, dtype=jnp.float32) / segment
    ).astype(jnp.bfloat16)
    land_q, land_k = (
        lax.all_gather(local_q, "seq", axis=0, tiled=True),
        lax.all_gather(local_k, "seq", axis=0, tiled=True),
    )
    query_landmark_means = land_q.reshape(M, H, DH)
    key_landmark_means = land_k.reshape(M, H, DH)
    query_heads_split = queries.reshape(tokens_here, H, DH)
    key_heads_split = keys.reshape(tokens_here, H, DH)
    value_heads_split = values.reshape(tokens_here, H, DH)
    start = position * owned
    local_query_block = lax.dynamic_slice_in_dim(query_landmark_means, start, owned, 1)
    local_key_block = lax.dynamic_slice_in_dim(key_landmark_means, start, owned, 1)
    kernel = softmax_last(
        jnp.einsum(
            "aft,eft->fae", local_query_block, local_key_block, preferred_element_type=jnp.float32
        )
        * score_scale
    )
    inverse = newton_schulz(kernel).astype(jnp.bfloat16)
    scores = (
        jnp.einsum(
            "luv,xuv->ulx",
            query_landmark_means,
            key_heads_split,
            preferred_element_type=jnp.float32,
        )
        * score_scale
    )
    local_peak = jnp.max(scores, -1)
    peak = lax.pmax(local_peak.astype(jnp.bfloat16), "seq").astype(local_peak.dtype)
    exponent_values = jnp.exp(scores - peak[..., None])
    totals = jnp.sum(exponent_values, -1)
    weighted = jnp.einsum(
        "fta,afr->ftr",
        exponent_values.astype(jnp.bfloat16),
        value_heads_split,
        preferred_element_type=jnp.float32,
    )
    totals, weighted = (totals, weighted)
    totals, weighted = (
        lax.psum_scatter(
            totals.astype(jnp.bfloat16), "seq", scatter_dimension=0, tiled=True
        ).astype(jnp.float32),
        lax.psum_scatter(
            weighted.astype(jnp.bfloat16), "seq", scatter_dimension=0, tiled=True
        ).astype(jnp.float32),
    )
    mine = (weighted / totals[..., None]).astype(jnp.bfloat16)
    own_product = jnp.einsum(
        "yco,yor->ycr", inverse, mine, preferred_element_type=jnp.float32
    ).astype(jnp.bfloat16)
    attention_product = lax.all_gather(own_product, "seq", axis=0, tiled=True)
    near = (
        jnp.einsum(
            "ivb,avb->via",
            query_heads_split,
            key_landmark_means,
            preferred_element_type=jnp.float32,
        )
        * score_scale
    )
    attention_weight = softmax_last(near).astype(jnp.bfloat16)
    result = jnp.einsum(
        "vcn,vnl->cvl", attention_weight, attention_product, preferred_element_type=jnp.float32
    ).astype(jnp.bfloat16)
    return result.reshape(tokens_here, D)


def solution(mesh):
    placed = (P(("doc", "seq"), None), P(("doc", "seq"), None), P(("doc", "seq"), None))
    return jax.shard_map(
        body, mesh=mesh, in_specs=placed, out_specs=P(("doc", "seq"), None), check_vma=False
    )
```

profile of v0, /device:TPU:0, one launch (start us, length us, event | category | flops | bytes accessed | tf_op | source)
XLA Modules:
  0.0 638.8 jit_solution(8765774548891744742)
XLA Ops:
  20.1 68.1 %all-gather.4.cloned.1.call-done = bf16[512,4096]{1,0:T(8,128)(2,1)} async-done(((bf16[64,4096]{1,0:T(8,128)(2,1)}), bf16[512,4096]{1,0:T(8,128)(2,1)}) %all-gather.4.cloned.1.call-update) | async-done | bytes 4194320 | tf_op jit(solution)/shard_map/all_gather | solution.py:52
  95.1 66.5 %all-gather.6.cloned.1.call-done = bf16[512,4096]{1,0:T(8,128)(2,1)} async-done(((bf16[64,4096]{1,0:T(8,128)(2,1)}), bf16[512,4096]{1,0:T(8,128)(2,1)}) %all-gather.6.cloned.1.call-update) | async-done | bytes 4194320 | tf_op jit(solution)/shard_map/all_gather | solution.py:53
  176.7 15.5 %multiply_reduce_fusion = (bf16[32,512]{1,0:T(8,128)(2,1)S(1)}, f32[32,512,512]{1,2,0:T(8,128)}) fusion(bf16[512,32,128]{0,2,1:T(8,128)(2,1)S(1)} %bitcast.76, bf16[512,4096]{1,0:T(8,128)(2,1)} %param.4), kind=kOutput, calls=%fused_computation.8 | convolution fusion | flops 2164244480 | bytes 41975808 | tf_op jit(solution)/shard_map/luv,xuv->ulx/dot_general | solution.py:71
  205.1 11.2 %online-softmax = f32[4,512,512]{2,1,0:T(8,128)} custom-call(f32[4,512,512]{2,1,0:T(8,128)} %convolution_multiply_fusion, f32[4,512,512]{2,1,0:T(8,128)} %copy.43), custom_call_target="tpu_custom_call" | custom-call | tf_op online-softmax
  216.4 10.9 %fusion.25 = f32[4,512,512]{2,1,0:T(8,128)S(1)} fusion(f32[4,512,512]{2,1,0:T(8,128)} %online-softmax, f32[512,512]{1,0:T(8,128)S(1)} %fusion.103), kind=kOutput, calls=%fused_computation.29 | convolution fusion | flops 6443499520 | bytes 9437184 | tf_op jit(solution)/shard_map/hij,hjk->hik/dot_general | solution.py:27
  243.7 11.4 %online-softmax.1 = f32[4,512,512]{2,1,0:T(8,128)} custom-call(f32[4,512,512]{2,1,0:T(8,128)} %convolution_multiply_fusion, f32[4,512,512]{2,1,0:T(8,128)} %fusion.65), custom_call_target="tpu_custom_call" | custom-call | tf_op online-softmax
  255.1 10.8 %fusion.23 = f32[4,512,512]{2,1,0:T(8,128)S(1)} fusion(f32[4,512,512]{2,1,0:T(8,128)} %online-softmax.1, f32[512,512]{1,0:T(8,128)S(1)} %fusion.103), kind=kOutput, calls=%fused_computation.27 | convolution fusion | flops 6443499520 | bytes 9437184 | tf_op jit(solution)/shard_map/hij,hjk->hik/dot_general | solution.py:27
  273.6 9.0 %fusion.68 = f32[4,512,512]{2,1,0:T(8,128)} fusion(f32[4,512,512]{2,1,0:T(8,128)S(1)} %copy-done.9, f32[4,512,512]{2,1,0:T(8,128)S(1)} %fusion.53, f32[512,512]{1,0:T(8,128)S(1)} %fusion.105), kind=kOutput, calls=%fused_computation.70 | convolution fusion | flops 6444548096 | bytes 13631488 | tf_op jit(solution)/shard_map/hij,hjk->hik/dot_general | solution.py:31
  282.5 11.2 %online-softmax.2 = f32[4,512,512]{2,1,0:T(8,128)} custom-call(f32[4,512,512]{2,1,0:T(8,128)} %convolution_multiply_fusion, f32[4,512,512]{2,1,0:T(8,128)} %fusion.68), custom_call_target="tpu_custom_call" | custom-call | tf_op online-softmax
  293.8 34.7 %pmax.7 = bf16[32,512]{1,0:T(8,128)(2,1)S(1)} all-reduce(bf16[32,512]{1,0:T(8,128)(2,1)S(1)} %get-tuple-element.9), channel_id=1, replica_groups=mesh['seq'=8,'doc'=4] {'seq'}, use_global_device_ids=true, to_apply=%region_9.0 | all-reduce | flops 16384 | bytes 65536 | tf_op jit(solution)/shard_map/pmax | solution.py:80
  328.5 16.6 %fusion.60 = bf16[32,512,128]{2,1,0:T(8,128)(2,1)} fusion(f32[32,512,512]{1,2,0:T(8,128)} %get-tuple-element.10, f32[32,512]{1,0:T(8,128)S(1)} %convert_element_type.69, bf16[512,4096]{1,0:T(8,128)(2,1)} %param.5), kind=kOutput, calls=%fused_computation.68 | convolution fusion | flops 2174746624 | bytes 42008576 | tf_op jit(solution)/shard_map/fta,afr->ftr/dot_general | solution.py:83
  345.2 10.9 %fusion.21 = f32[4,512,512]{2,1,0:T(8,128)S(1)} fusion(f32[4,512,512]{2,1,0:T(8,128)} %online-softmax.2, f32[512,512]{1,0:T(8,128)S(1)} %fusion.103), kind=kOutput, calls=%fused_computation.25 | convolution fusion | flops 6443499520 | bytes 9437184 | tf_op jit(solution)/shard_map/hij,hjk->hik/dot_general | solution.py:27
  372.6 11.3 %online-softmax.3 = f32[4,512,512]{2,1,0:T(8,128)} custom-call(f32[4,512,512]{2,1,0:T(8,128)} %convolution_multiply_fusion, f32[4,512,512]{2,1,0:T(8,128)} %fusion.71), custom_call_target="tpu_custom_call" | custom-call | tf_op online-softmax
  383.8 11.2 %fusion.19 = f32[4,512,512]{2,1,0:T(8,128)S(1)} fusion(f32[4,512,512]{2,1,0:T(8,128)} %online-softmax.3, f32[512,512]{1,0:T(8,128)S(1)} %fusion.103), kind=kOutput, calls=%fused_computation.23 | convolution fusion | flops 6443499520 | bytes 9437184 | tf_op jit(solution)/shard_map/hij,hjk->hik/dot_general | solution.py:27
  411.3 11.2 %online-softmax.4 = f32[4,512,512]{2,1,0:T(8,128)} custom-call(f32[4,512,512]{2,1,0:T(8,128)} %convolution_multiply_fusion, f32[4,512,512]{2,1,0:T(8,128)} %fusion.74), custom_call_target="tpu_custom_call" | custom-call | tf_op online-softmax
  422.5 10.9 %fusion.17 = f32[4,512,512]{2,1,0:T(8,128)S(1)} fusion(f32[4,512,512]{2,1,0:T(8,128)} %online-softmax.4, f32[512,512]{1,0:T(8,128)S(1)} %fusion.103), kind=kOutput, calls=%fused_computation.21 | convolution fusion | flops 6443499520 | bytes 9437184 | tf_op jit(solution)/shard_map/hij,hjk->hik/dot_general | solution.py:27
  449.7 11.2 %online-softmax.5 = f32[4,512,512]{2,1,0:T(8,128)} custom-call(f32[4,512,512]{2,1,0:T(8,128)} %convolution_multiply_fusion, f32[4,512,512]{2,1,0:T(8,128)} %fusion.77), custom_call_target="tpu_custom_call" | custom-call | tf_op online-softmax
  460.9 13.6 %fusion.5 = bf16[32,512]{1,0:T(8,128)(2,1)S(1)} fusion(f32[32,512,512]{1,2,0:T(8,128)} %get-tuple-element.10, f32[32,512]{1,0:T(8,128)S(1)} %convert_element_type.69), kind=kLoop, calls=%fused_computation.10 | loop fusion | flops 25149440 | bytes 33652736 | tf_op jit(solution)/shard_map/reduce_sum | solution.py:82
  474.5 33.4 %all-reduce = bf16[32,512]{1,0:T(8,128)(2,1)S(1)} all-reduce(bf16[32,512]{1,0:T(8,128)(2,1)S(1)} %fusion.5), channel_id=3, replica_groups=mesh['seq'=8,'doc'=4] {'seq'}, use_global_device_ids=true, to_apply=%region_12.0.clone | all-reduce | flops 16384 | bytes 65536
  508.0 10.8 %fusion.15 = f32[4,512,512]{2,1,0:T(8,128)S(1)} fusion(f32[4,512,512]{2,1,0:T(8,128)} %online-softmax.5, f32[512,512]{1,0:T(8,128)S(1)} %fusion.103), kind=kOutput, calls=%fused_computation.19 | convolution fusion | flops 6443499520 | bytes 9437184 | tf_op jit(solution)/shard_map/hij,hjk->hik/dot_general | solution.py:27
  539.1 19.2 %fusion.27 = f32[32,512,512]{1,2,0:T(8,128)} fusion(bf16[512,32,128]{0,2,1:T(8,128)(2,1)} %bitcast.73, bf16[512,4096]{1,0:T(8,128)(2,1)} %param.3), kind=kOutput, calls=%fused_computation.31 | convolution fusion | flops 2147483648 | bytes 41943040 | tf_op jit(solution)/shard_map/ivb,avb->via/dot_general | solution.py:104
  558.3 37.1 %fusion.125 = (f32[32,512]{1,0:T(8,128)S(1)}, f32[32,512,512]{2,1,0:T(8,128)}) fusion(f32[32,512,512]{1,2,0:T(8,128)} %fusion.27), kind=kOutput, calls=%fused_computation.116 | output fusion | flops 33554944 | bytes 67174400 | tf_op jit(solution)/shard_map/sub | solution.py:15
  595.4 13.9 %all-gather.8.cloned.1.call-done = bf16[32,512,128]{2,1,0:T(8,128)(2,1)} async-done(((bf16[4,512,128]{2,1,0:T(8,128)(2,1)}), bf16[32,512,128]{2,1,0:T(8,128)(2,1)}) %all-gather.8.cloned.1.call-update) | async-done | bytes 4194320 | tf_op jit(solution)/shard_map/all_gather | solution.py:102
  609.3 16.5 %fusion.59 = bf16[32,128,512]{2,1,0:T(8,128)(2,1)} fusion(bf16[32,512,128]{2,1,0:T(8,128)(2,1)} %all-gather.8.cloned.1.call-done, f32[32,512,512]{2,1,0:T(8,128)} %get-tuple-element.12, f32[32,512]{1,0:T(8,128)S(1)} %get-tuple-element.11), kind=kOutput, calls=%fused_computation.67 | convolution fusion | flops 2166358016 | bytes 42008576 | tf_op jit(solution)/shard_map/vcn,vnl->cvl/dot_general | solution.py:113
  (70 shorter events, 147.4 us)
Async XLA Ops:
  6.5 81.6 %all-gather.4.cloned.1.call-start = ((), (), s32[]{:S(2)}) async-start(), calls=%async_computation.1 | async-start | bytes 4718592 | tf_op jit(solution)/shard_map/all_gather | solution.py:52
  12.5 6.0 copy-start.13
  12.5 149.2 %all-gather.6.cloned.1.call-start = ((), (), s32[]{:S(2)}) async-start(), calls=%async_computation.2 | async-start | bytes 4718592 | tf_op jit(solution)/shard_map/all_gather | solution.py:53
  18.4 516.7 %reduce-scatter.2.cloned.1.call-start = ((), (), s32[]{:S(2)}) async-start(), calls=%async_computation.3 | async-start | bytes 4718592 | tf_op jit(solution)/shard_map/reduce_scatter | solution.py:94
  172.6 4.1 copy-start.12
  216.4 10.9 %copy-start.2 = (f32[4,512,512]{2,1,0:T(8,128)S(1)}, f32[4,512,512]{2,1,0:T(8,128)}, u32[]{:S(2)}) copy-start(f32[4,512,512]{2,1,0:T(8,128)} %online-softmax) | copy-start | bytes 12582916
  227.3 7.7 %copy-start.8 = (f32[4,512,512]{1,2,0:T(8,128)S(1)}, f32[4,512,512]{1,2,0:T(8,128)}, u32[]{:S(2)}) copy-start(f32[4,512,512]{1,2,0:T(8,128)} %bitcast_divide_fusion) | copy-start | bytes 12582916
  255.1 10.8 %copy-start.3 = (f32[4,512,512]{2,1,0:T(8,128)S(1)}, f32[4,512,512]{2,1,0:T(8,128)}, u32[]{:S(2)}) copy-start(f32[4,512,512]{2,1,0:T(8,128)} %online-softmax.1) | copy-start | bytes 12582916
  265.9 7.7 %copy-start.9 = (f32[4,512,512]{2,1,0:T(8,128)S(1)}, f32[4,512,512]{2,1,0:T(8,128)}, u32[]{:S(2)}) copy-start(f32[4,512,512]{2,1,0:T(8,128)} %fusion.65) | copy-start | bytes 12582916
  345.1 264.2 %all-gather.8.cloned.1.call-start = ((), (), s32[]{:S(2)}) async-start(), calls=%async_computation.4 | async-start | bytes 4718592 | tf_op jit(solution)/shard_map/all_gather | solution.py:102
  345.2 11.0 %copy-start = (f32[4,512,512]{2,1,0:T(8,128)S(1)}, f32[4,512,512]{2,1,0:T(8,128)}, u32[]{:S(2)}) copy-start(f32[4,512,512]{2,1,0:T(8,128)} %online-softmax.2) | copy-start | bytes 12582916
  356.1 7.7 %copy-start.6 = (f32[4,512,512]{2,1,0:T(8,128)S(1)}, f32[4,512,512]{2,1,0:T(8,128)}, u32[]{:S(2)}) copy-start(f32[4,512,512]{2,1,0:T(8,128)} %fusion.68) | copy-start | bytes 12582916
  383.8 11.2 %copy-start.4 = (f32[4,512,512]{2,1,0:T(8,128)S(1)}, f32[4,512,512]{2,1,0:T(8,128)}, u32[]{:S(2)}) copy-start(f32[4,512,512]{2,1,0:T(8,128)} %online-softmax.3) | copy-start | bytes 12582916
  395.1 7.7 %copy-start.10 = (f32[4,512,512]{2,1,0:T(8,128)S(1)}, f32[4,512,512]{2,1,0:T(8,128)}, u32[]{:S(2)}) copy-start(f32[4,512,512]{2,1,0:T(8,128)} %fusion.71) | copy-start | bytes 12582916
  422.5 10.9 %copy-start.5 = (f32[4,512,512]{2,1,0:T(8,128)S(1)}, f32[4,512,512]{2,1,0:T(8,128)}, u32[]{:S(2)}) copy-start(f32[4,512,512]{2,1,0:T(8,128)} %online-softmax.4) | copy-start | bytes 12582916
  433.5 7.7 %copy-start.11 = (f32[4,512,512]{2,1,0:T(8,128)S(1)}, f32[4,512,512]{2,1,0:T(8,128)}, u32[]{:S(2)}) copy-start(f32[4,512,512]{2,1,0:T(8,128)} %fusion.74) | copy-start | bytes 12582916
  508.0 10.8 %copy-start.1 = (f32[4,512,512]{2,1,0:T(8,128)S(1)}, f32[4,512,512]{2,1,0:T(8,128)}, u32[]{:S(2)}) copy-start(f32[4,512,512]{2,1,0:T(8,128)} %online-softmax.5) | copy-start | bytes 12582916
  518.8 7.7 %copy-start.7 = (f32[4,512,512]{2,1,0:T(8,128)S(1)}, f32[4,512,512]{2,1,0:T(8,128)}, u32[]{:S(2)}) copy-start(f32[4,512,512]{2,1,0:T(8,128)} %fusion.77) | copy-start | bytes 12582916
Sparse Core Ops, SparseCore 0:
  12.6 75.5 all-gather.3
  90.3 71.3 all-gather.5
  345.2 85.5 reduce-scatter.1
  539.2 70.0 all-gather.7
where the time goes:
time: 645 us; the launch traced here: 639 us
  matrix products  244 us (38%)
  waiting for transfers between devices  149 us (23%)
  other arithmetic  70.6 us (11%)
  blocking collectives  68.2 us (11%)
  Pallas kernels  67.7 us (10%)
  local copies, waits for them, and re-layouts  25.6 us (4%)
  between operations  14.3 us (2%)
    all_gather x1, waiting for transfers between devices, body(): lax.all_gather(local_q, 'seq', axis=0, tiled=True)  68.1 us
    unnamed x6, Pallas kernels  67.7 us
    all_gather x1, waiting for transfers between devices, body(): lax.all_gather(local_k, 'seq', axis=0, tiled=True)  66.5 us
    dot_general x6, matrix products, newton_schulz(): jnp.einsum('hij,hjk->hik', kernel_inv, 7.0 * identity - kernel_inv, preci...  65.6 us
    dot_general x6, matrix products, newton_schulz(): jnp.einsum('hij,hjk->hik', inverse, 13.0 * identity - middle, precision=p...  52.2 us
    dot_general x6, matrix products, newton_schulz(): jnp.einsum('hij,hjk->hik', kernel_inv, 15.0 * identity - inner, precision...  45.8 us
    sub x1, other arithmetic, softmax_last(): exponent_values = jnp.exp(scores - top)  37.1 us
    pmax x1, blocking collectives, body(): lax.pmax(local_peak.astype(jnp.bfloat16), 'seq').astype(local_peak.dtype)  34.7 us
  transfers between devices with their start and end apart: 4, of which 3 were waited for; matrix products, arithmetic and copies ran while one was open for 30% of the time, Pallas kernels for 5%

commit v1 on v0

v1 whole, which is shorter than its diff:
```python
import functools

import jax
import jax.numpy as jnp
from jax import lax
from jax.experimental import pallas as pl
from jax.experimental.pallas import tpu as pltpu
from jax.sharding import PartitionSpec as P

H = 32
DH = 128
M = 512
ITERS = 6
F32 = jnp.float32
BF16 = jnp.bfloat16
PAD = 16
SCALE = DH ** (-0.5)
VMEM_LIMIT = 60 * 1024 * 1024


def dot(a, b, dims):
    return lax.dot_general(a, b, (dims, ((), ())), preferred_element_type=F32)


NN = ((1,), (0,))
NT = ((1,), (1,))
TN = ((0,), (0,))


def cost(flops, nbytes, trans=0):
    return pl.CostEstimate(flops=int(flops), bytes_accessed=int(nbytes), transcendentals=int(trans))


def params(axes=1):
    return pltpu.CompilerParams(dimension_semantics=("arbitrary",) * axes, vmem_limit_bytes=VMEM_LIMIT)


def means_kernel(segment, x_ref, o_ref):
    rows, tokens = o_ref.shape[0], x_ref.shape[0]
    row = lax.broadcasted_iota(jnp.int32, (rows, tokens), 0)
    col = lax.broadcasted_iota(jnp.int32, (rows, tokens), 1)
    inside = jnp.logical_and(col >= row * segment, col < (row + 1) * segment)
    pick = jnp.where(inside, 1.0, 0.0).astype(BF16)
    o_ref[...] = (dot(pick, x_ref[...], NN) / segment).astype(BF16)


def means(x, rows):
    tokens, width = x.shape
    block = min(width, 1024)
    return pl.pallas_call(
        functools.partial(means_kernel, tokens // rows),
        grid=(width // block,),
        in_specs=[pl.BlockSpec((tokens, block), lambda i: (0, i))],
        out_specs=pl.BlockSpec((rows, block), lambda i: (0, i)),
        out_shape=jax.ShapeDtypeStruct((rows, width), BF16),
        compiler_params=params(),
        cost_estimate=cost(2 * rows * tokens * width, 2 * tokens * width),
        name="means",
    )(x)


def peaks_kernel(lq_ref, k_ref, o_ref):
    scores = dot(k_ref[...], lq_ref[...], NT) * SCALE
    o_ref[0] = jnp.max(scores, 0, keepdims=True)


def peaks(land_q, keys):
    tokens = keys.shape[0]
    return pl.pallas_call(
        peaks_kernel,
        grid=(H,),
        in_specs=[
            pl.BlockSpec((M, DH), lambda h: (0, h)),
            pl.BlockSpec((tokens, DH), lambda h: (0, h)),
        ],
        out_specs=pl.BlockSpec((1, 1, M), lambda h: (h, 0, 0)),
        out_shape=jax.ShapeDtypeStruct((H, 1, M), F32),
        compiler_params=params(),
        cost_estimate=cost(4 * H * tokens * M * DH, 4 * tokens * H * DH),
        name="peaks",
    )(land_q, keys)


def exchange_kernel(n, x_ref, o_ref, held, send_sem, recv_sem):
    me = lax.axis_index("seq")
    barrier = pltpu.get_barrier_semaphore()
    for step in range(1, n):
        pl.semaphore_signal(
            barrier, inc=1, device_id={"seq": lax.rem(me + step, n)}, device_id_type=pl.DeviceIdType.MESH
        )
    pl.semaphore_wait(barrier, n - 1)
    copies = []
    for step in range(1, n):
        copy = pltpu.make_async_remote_copy(
            src_ref=x_ref,
            dst_ref=held.at[step - 1],
            send_sem=send_sem.at[step - 1],
            recv_sem=recv_sem.at[step - 1],
            device_id={"seq": lax.rem(me + step, n)},
            device_id_type=pl.DeviceIdType.MESH,
        )
        copy.start()
        copies.append(copy)
    for copy in copies:
        copy.wait()
    best = x_ref[...]
    for step in range(1, n):
        best = jnp.maximum(best, held[step - 1])
    o_ref[...] = best


def exchange_max(x, n):
    return pl.pallas_call(
        functools.partial(exchange_kernel, n),
        in_specs=[pl.BlockSpec(memory_space=pltpu.VMEM)],
        out_specs=pl.BlockSpec(memory_space=pltpu.VMEM),
        out_shape=jax.ShapeDtypeStruct(x.shape, x.dtype),
        scratch_shapes=[
            pltpu.VMEM((n - 1,) + x.shape, x.dtype),
            pltpu.SemaphoreType.DMA((n - 1,)),
            pltpu.SemaphoreType.DMA((n - 1,)),
        ],
        compiler_params=pltpu.CompilerParams(collective_id=0, has_side_effects=True),
        name="exchange_max",
    )(x)


def weighted_kernel(lq_ref, k_ref, v_ref, peak_ref, o_ref):
    scores = dot(k_ref[...], lq_ref[...], NT) * SCALE
    expo = jnp.exp(scores - peak_ref[0])
    totals = jnp.sum(expo, 0, keepdims=True)
    o_ref[0, :DH, :] = dot(v_ref[...], expo.astype(BF16), TN).astype(BF16)
    o_ref[0, DH:, :] = jnp.broadcast_to(totals, (PAD, totals.shape[1])).astype(BF16)


def weighted_sums(land_q, keys, values, peak):
    tokens = keys.shape[0]
    return pl.pallas_call(
        weighted_kernel,
        grid=(H,),
        in_specs=[
            pl.BlockSpec((M, DH), lambda h: (0, h)),
            pl.BlockSpec((tokens, DH), lambda h: (0, h)),
            pl.BlockSpec((tokens, DH), lambda h: (0, h)),
            pl.BlockSpec((1, 1, M), lambda h: (h, 0, 0)),
        ],
        out_specs=pl.BlockSpec((1, DH + PAD, M), lambda h: (h, 0, 0)),
        out_shape=jax.ShapeDtypeStruct((H, DH + PAD, M), BF16),
        compiler_params=params(),
        cost_estimate=cost(8 * H * tokens * M * DH, 8 * tokens * H * DH, H * tokens * M),
        name="weighted",
    )(land_q, keys, values, peak)


def inverse_kernel(heads, pos_ref, lq_ref, lk_ref, o_ref, kern, z_ref):
    row = lax.broadcasted_iota(jnp.int32, (M, M), 0)
    col = lax.broadcasted_iota(jnp.int32, (M, M), 1)
    eye = row == col
    for h in range(heads):
        cols = slice(h * DH, (h + 1) * DH)
        scores = dot(lq_ref[:, cols], lk_ref[:, cols], NT) * SCALE
        expo = jnp.exp(scores - jnp.max(scores, 1, keepdims=True))
        kernel = expo / jnp.sum(expo, 1, keepdims=True)
        row_most = jnp.max(jnp.sum(kernel, 1, keepdims=True), 0, keepdims=True)
        col_most = jnp.max(jnp.sum(kernel, 0, keepdims=True), 1, keepdims=True)
        kern[h] = kernel.astype(BF16)
        z_ref[h] = kernel.T / (row_most * col_most)

    def sweep(i, carry):
        zs = [z_ref[h] for h in range(heads)]
        low = [z.astype(BF16) for z in zs]
        p = [dot(kern[h], low[h], NN) for h in range(heads)]
        pb = [x.astype(BF16) for x in p]
        q1 = [dot(pb[h], jnp.where(eye, 7.0 - p[h], -p[h]).astype(BF16), NN) for h in range(heads)]
        q2 = [dot(pb[h], jnp.where(eye, 15.0 - q1[h], -q1[h]).astype(BF16), NN) for h in range(heads)]
        for h in range(heads):
            z_ref[h] = 0.25 * dot(low[h], jnp.where(eye, 13.0 - q2[h], -q2[h]).astype(BF16), NN)
        return carry

    lax.fori_loop(0, ITERS, sweep, 0)
    for h in range(heads):
        o_ref[h] = z_ref[h].astype(BF16)


def inverses(land_q, land_k, position, owned):
    heads = 2 if owned % 2 == 0 else 1
    steps = owned // heads
    return pl.pallas_call(
        functools.partial(inverse_kernel, heads),
        grid_spec=pltpu.PrefetchScalarGridSpec(
            num_scalar_prefetch=1,
            grid=(steps,),
            in_specs=[
                pl.BlockSpec((M, heads * DH), lambda i, pos: (0, pos[0] * steps + i)),
                pl.BlockSpec((M, heads * DH), lambda i, pos: (0, pos[0] * steps + i)),
            ],
            out_specs=pl.BlockSpec((heads, M, M), lambda i, pos: (i, 0, 0)),
            scratch_shapes=[pltpu.VMEM((heads, M, M), BF16), pltpu.VMEM((heads, M, M), F32)],
        ),
        out_shape=jax.ShapeDtypeStruct((owned, M, M), BF16),
        compiler_params=params(),
        cost_estimate=cost(owned * ITERS * 8 * M * M * M, 4 * owned * M * M),
        name="inverse",
    )(position.reshape(1).astype(jnp.int32), land_q, land_k)


def product_kernel(inv_ref, w_ref, o_ref):
    w = w_ref[0].astype(F32)
    normed = (w[:DH] / w[DH : DH + 1]).astype(BF16)
    o_ref[0] = dot(inv_ref[0], normed, NT).astype(BF16)


def products(inverse, summed):
    owned = inverse.shape[0]
    return pl.pallas_call(
        product_kernel,
        grid=(owned,),
        in_specs=[
            pl.BlockSpec((1, M, M), lambda h: (h, 0, 0)),
            pl.BlockSpec((1, DH + PAD, M), lambda h: (h, 0, 0)),
        ],
        out_specs=pl.BlockSpec((1, M, DH), lambda h: (h, 0, 0)),
        out_shape=jax.ShapeDtypeStruct((owned, M, DH), BF16),
        compiler_params=params(),
        cost_estimate=cost(4 * owned * M * M * DH, 2 * owned * M * M),
        name="product",
    )(inverse, summed)


def weights_kernel(q_ref, lk_ref, o_ref):
    scores = dot(q_ref[...], lk_ref[...], NT) * SCALE
    expo = jnp.exp(scores - jnp.max(scores, 1, keepdims=True))
    o_ref[0] = (expo / jnp.sum(expo, 1, keepdims=True)).astype(BF16)


def token_weights(queries, land_k):
    tokens = queries.shape[0]
    return pl.pallas_call(
        weights_kernel,
        grid=(H,),
        in_specs=[
            pl.BlockSpec((tokens, DH), lambda h: (0, h)),
            pl.BlockSpec((M, DH), lambda h: (0, h)),
        ],
        out_specs=pl.BlockSpec((1, tokens, M), lambda h: (h, 0, 0)),
        out_shape=jax.ShapeDtypeStruct((H, tokens, M), BF16),
        compiler_params=params(),
        cost_estimate=cost(4 * H * tokens * M * DH, 2 * H * tokens * M, H * tokens * M),
        name="weights",
    )(queries, land_k)


def attend_kernel(w_ref, p_ref, o_ref):
    o_ref[...] = dot(w_ref[0], p_ref[0], NN).astype(BF16)


def attend(weights, product):
    tokens = weights.shape[1]
    return pl.pallas_call(
        attend_kernel,
        grid=(H,),
        in_specs=[
            pl.BlockSpec((1, tokens, M), lambda h: (h, 0, 0)),
            pl.BlockSpec((1, M, DH), lambda h: (h, 0, 0)),
        ],
        out_specs=pl.BlockSpec((tokens, DH), lambda h: (0, h)),
        out_shape=jax.ShapeDtypeStruct((tokens, H * DH), BF16),
        compiler_params=params(),
        cost_estimate=cost(4 * H * tokens * M * DH, 2 * H * tokens * M),
        name="attend",
    )(weights, product)


def body(queries, keys, values):
    devices = lax.axis_size("seq")
    position = lax.axis_index("seq")
    per_device = M // devices
    owned = H // devices
    local_q = means(queries, per_device)
    local_k = means(keys, per_device)
    land_q = lax.all_gather(local_q, "seq", axis=0, tiled=True)
    land_k = lax.all_gather(local_k, "seq", axis=0, tiled=True)
    peak = exchange_max(peaks(land_q, keys), devices)
    partial = weighted_sums(land_q, keys, values, peak)
    summed = lax.psum_scatter(partial, "seq", scatter_dimension=0, tiled=True)
    inverse = inverses(land_q, land_k, position, owned)
    own_product = products(inverse, summed)
    product = lax.all_gather(own_product, "seq", axis=0, tiled=True)
    weights = token_weights(queries, land_k)
    return attend(weights, product)


def solution(mesh):
    placed = (P(("doc", "seq"), None),) * 3
    return jax.shard_map(
        body, mesh=mesh, in_specs=placed, out_specs=P(("doc", "seq"), None), check_vma=False
    )
```

time: 645 us -> 375 us (0.58)
  matrix products: 244 us -> 0 us
  Pallas kernels: 67.7 us -> 167 us
  other arithmetic: 70.6 us -> 0 us
  blocking collectives: 68.2 us -> 0 us
  waiting for transfers between devices: 149 us -> 192 us
  local copies, waits for them, and re-layouts: 25.6 us -> 0 us
    dot_general x24 -> x0, matrix products: 239 us -> none  [the longest x6 65.6 us: newton_schulz(): jnp.einsum('hij,hjk->hik', kernel_inv, 7.0 * identity - kernel_inv, preci...]
    pallas_call x0 -> x9, Pallas kernels: none -> 167 us  [the longest x1 33.8 us: inverses(): pl.pallas_call(functools.partial(inverse_kernel, heads), grid_spec=pltpu....]
    unnamed x6 -> x0, Pallas kernels: 67.7 us -> none
    reduce_scatter x1, waiting for transfers between devices: 0.01 us -> 64.1 us  [body(): summed = lax.psum_scatter(partial, 'seq', scatter_dimension=0, tiled=True)]
    sub x1 -> x0, other arithmetic: 37.1 us -> none  [softmax_last(): exponent_values = jnp.exp(scores - top)]
    pmax x1 -> x0, blocking collectives: 34.7 us -> none  [body(): lax.pmax(local_peak.astype(jnp.bfloat16), 'seq').astype(local_peak.dtype)]
    unnamed x1 -> x0, blocking collectives: 33.4 us -> none
    reduce_sum x4 -> x0, other arithmetic: 26.6 us -> none  [the longest x1 13.6 us: body(): totals = jnp.sum(exponent_values, -1)]
  transfers between devices with their start and end apart: 4 -> 4, of which waited for: 3 -> 4; matrix products, arithmetic and copies ran while one was open for 30% -> 0% of each run, Pallas kernels for 5% -> 36%
where the time goes in v1:
time: 375 us; the launch traced here: 373 us
  waiting for transfers between devices  192 us (51%)
  Pallas kernels  167 us (45%)
  between operations  13.1 us (3%)
    all_gather x1, waiting for transfers between devices, body(): land_q = lax.all_gather(local_q, 'seq', axis=0, tiled=True)  71.1 us
    reduce_scatter x1, waiting for transfers between devices, body(): summed = lax.psum_scatter(partial, 'seq', scatter_dimension=0, tiled=True)  64.1 us
    all_gather x1, waiting for transfers between devices, body(): product = lax.all_gather(own_product, 'seq', axis=0, tiled=True)  43.4 us
    pallas_call x1, Pallas kernels, inverses(): pl.pallas_call(functools.partial(inverse_kernel, heads), grid_spec=pltpu....  33.8 us
    pallas_call x1, Pallas kernels, token_weights(): pl.pallas_call(weights_kernel, grid=(H,), in_specs=[pl.BlockSpec((tokens,...  29.2 us
    pallas_call x1, Pallas kernels, weighted_sums(): pl.pallas_call(weighted_kernel, grid=(H,), in_specs=[pl.BlockSpec((M, DH)...  28 us
    pallas_call x1, Pallas kernels, attend(): pl.pallas_call(attend_kernel, grid=(H,), in_specs=[pl.BlockSpec((1, token...  24.6 us
    pallas_call x1, Pallas kernels, peaks(): pl.pallas_call(peaks_kernel, grid=(H,), in_specs=[pl.BlockSpec((M, DH), l...  22.4 us
  transfers between devices with their start and end apart: 4, of which 4 were waited for; matrix products, arithmetic and copies ran while one was open for 0% of the time, Pallas kernels for 36%

profile of v1, /device:TPU:0, one launch (start us, length us, event | category | flops | bytes accessed | tf_op | source)
XLA Modules:
  0.0 372.6 jit_solution(54103869907430294)
XLA Ops:
  6.5 0.0 all-gather.6.cloned.1.call-start
  6.5 4.5 %means.3 = bf16[64,4096]{1,0:T(8,128)(2,1)} custom-call(bf16[512,4096]{1,0:T(8,128)(2,1)} %x_ref.3), custom_call_target="tpu_custom_call" | custom-call | flops 268435456 | bytes 4194304 | tf_op jit(solution)/shard_map/means/pallas_call | solution.py:50
  11.0 0.0 all-gather.6.cloned.1.call-update
  11.1 0.0 all-gather.4.cloned.1.call-start
  11.1 4.5 %means.2 = bf16[64,4096]{1,0:T(8,128)(2,1)} custom-call(bf16[512,4096]{1,0:T(8,128)(2,1)} %k_ref.3), custom_call_target="tpu_custom_call" | custom-call | flops 268435456 | bytes 4194304 | tf_op jit(solution)/shard_map/means/pallas_call | solution.py:50
  15.6 0.0 all-gather.4.cloned.1.call-update
  15.6 0.0 reduce-scatter.2.cloned.1.call-start
  15.6 71.1 %all-gather.6.cloned.1.call-done.lq_ref = bf16[512,4096]{1,0:T(8,128)(2,1)} async-done(((bf16[64,4096]{1,0:T(8,128)(2,1)}), bf16[512,4096]{1,0:T(8,128)(2,1)}) %all-gather.6.cloned.1.call-update) | async-done | bytes 4194320 | tf_op jit(solution)/shard_map/all_gather | solution.py:281
  86.7 22.4 %peaks.1.x_ref = f32[32,1,512]{2,1,0:T(1,128)} custom-call(bf16[512,4096]{1,0:T(8,128)(2,1)} %all-gather.6.cloned.1.call-done.lq_ref, bf16[512,4096]{1,0:T(8,128)(2,1)} %k_ref.3), custom_call_target="tpu_custom_call" | custom-call | flops 4294967296 | bytes 8388608 | tf_op jit(solution)/shard_map/peaks/pallas_call | solution.py:69
  109.1 16.1 %exchange_max.1.peak_ref = f32[32,1,512]{2,1,0:T(1,128)} custom-call(f32[32,1,512]{2,1,0:T(1,128)} %peaks.1.x_ref), custom_call_target="tpu_custom_call" | custom-call | tf_op jit(solution)/shard_map/exchange_max/pallas_call | solution.py:113
  125.2 28.0 %weighted.1 = bf16[32,144,512]{2,1,0:T(8,128)(2,1)} custom-call(bf16[512,4096]{1,0:T(8,128)(2,1)} %all-gather.6.cloned.1.call-done.lq_ref, bf16[512,4096]{1,0:T(8,128)(2,1)} %k_ref.3, bf16[512,4096]{1,0:T(8,128)(2,1)} %v_ref.1, f32[32,1,512]{2,1,0:T(1,128)} %exchange_max.1.peak_ref), custom_call_target="tpu_custom_call" | custom-call | flops 8589934592 | bytes 16777216 | tf_op jit(solution)/shard_map/weighted/pallas_call | solution.py:138
  153.2 0.0 reduce-scatter.2.cloned.1.call-update
  153.2 0.0 all-gather.8.cloned.1.call-start
  153.3 13.6 %all-gather.4.cloned.1.call-done.lk_ref = bf16[512,4096]{1,0:T(8,128)(2,1)} async-done(((bf16[64,4096]{1,0:T(8,128)(2,1)}), bf16[512,4096]{1,0:T(8,128)(2,1)}) %all-gather.4.cloned.1.call-update) | async-done | bytes 4194320 | tf_op jit(solution)/shard_map/all_gather | solution.py:282
  166.9 33.8 %inverse.1.inv_ref = bf16[4,512,512]{2,1,0:T(8,128)(2,1)} custom-call(s32[1]{0:T(128)} %bitcast.pos_ref, bf16[512,4096]{1,0:T(8,128)(2,1)} %all-gather.6.cloned.1.call-done.lq_ref, bf16[512,4096]{1,0:T(8,128)(2,1)} %all-gather.4.cloned.1.call-done.lk_ref), custom_call_target="tpu_custom_call" | custom-call | flops 25769803776 | bytes 4194304 | tf_op jit(solution)/shard_map/inverse/pallas_call | solution.py:188
  200.7 64.1 %reduce-scatter.2.cloned.1.call-done.w_ref = bf16[4,144,512]{2,1,0:T(8,128)(2,1)} async-done(((bf16[32,144,512]{2,1,0:T(8,128)(2,1)}), bf16[4,144,512]{2,1,0:T(8,128)(2,1)}) %reduce-scatter.2.cloned.1.call-update) | async-done | bytes 589840 | tf_op jit(solution)/shard_map/reduce_scatter | solution.py:285
  264.7 4.1 %product.1 = bf16[4,512,128]{2,1,0:T(8,128)(2,1)} custom-call(bf16[4,512,512]{2,1,0:T(8,128)(2,1)} %inverse.1.inv_ref, bf16[4,144,512]{2,1,0:T(8,128)(2,1)} %reduce-scatter.2.cloned.1.call-done.w_ref), custom_call_target="tpu_custom_call" | custom-call | flops 536870912 | bytes 2097152 | tf_op jit(solution)/shard_map/product/pallas_call | solution.py:215
  268.8 0.0 all-gather.8.cloned.1.call-update
  268.9 29.2 %weights.1.w_ref = bf16[32,512,512]{2,1,0:T(8,128)(2,1)} custom-call(bf16[512,4096]{1,0:T(8,128)(2,1)} %x_ref.3, bf16[512,4096]{1,0:T(8,128)(2,1)} %all-gather.4.cloned.1.call-done.lk_ref), custom_call_target="tpu_custom_call" | custom-call | flops 4294967296 | bytes 16777216 | tf_op jit(solution)/shard_map/weights/pallas_call | solution.py:238
  298.1 43.4 %all-gather.8.cloned.1.call-done.p_ref = bf16[32,512,128]{2,1,0:T(8,128)(2,1)} async-done(((bf16[4,512,128]{2,1,0:T(8,128)(2,1)}), bf16[32,512,128]{2,1,0:T(8,128)(2,1)}) %all-gather.8.cloned.1.call-update) | async-done | bytes 4194320 | tf_op jit(solution)/shard_map/all_gather | solution.py:288
  341.5 24.6 %attend.1 = bf16[512,4096]{1,0:T(8,128)(2,1)} custom-call(bf16[32,512,512]{2,1,0:T(8,128)(2,1)} %weights.1.w_ref, bf16[32,512,128]{2,1,0:T(8,128)(2,1)} %all-gather.8.cloned.1.call-done.p_ref), custom_call_target="tpu_custom_call" | custom-call | flops 4294967296 | bytes 16777216 | tf_op jit(solution)/shard_map/attend/pallas_call | solution.py:259
Async XLA Ops:
  6.5 80.2 %all-gather.6.cloned.1.call-start = ((), (), s32[]{:S(2)}) async-start(), calls=%async_computation.2 | async-start | bytes 4718592 | tf_op jit(solution)/shard_map/all_gather | solution.py:281
  11.1 155.8 %all-gather.4.cloned.1.call-start = ((), (), s32[]{:S(2)}) async-start(), calls=%async_computation.1 | async-start | bytes 4718592 | tf_op jit(solution)/shard_map/all_gather | solution.py:282
  15.6 249.2 %reduce-scatter.2.cloned.1.call-start = ((), (), s32[]{:S(2)}) async-start(), calls=%async_computation.3 | async-start | bytes 5308416 | tf_op jit(solution)/shard_map/reduce_scatter | solution.py:285
  153.2 188.3 %all-gather.8.cloned.1.call-start = ((), (), s32[]{:S(2)}) async-start(), calls=%async_computation.4 | async-start | bytes 4718592 | tf_op jit(solution)/shard_map/all_gather | solution.py:288
Sparse Core Ops, SparseCore 0:
  11.2 75.4 all-gather.5
  88.9 77.9 all-gather.3
  170.5 94.1 reduce-scatter.1
  269.0 72.4 all-gather.7

commit v2 on v1

v2 whole, which is shorter than its diff:
```python
import functools

import jax
import jax.numpy as jnp
from jax import lax
from jax.experimental import pallas as pl
from jax.experimental.pallas import tpu as pltpu
from jax.sharding import PartitionSpec as P

H = 32
DH = 128
M = 512
ITERS = 6
F32 = jnp.float32
BF16 = jnp.bfloat16
SCALE = DH ** (-0.5)
MESH = pl.DeviceIdType.MESH
VMEM_LIMIT = 60 * 1024 * 1024


def dot(a, b, dims):
    return lax.dot_general(a, b, (dims, ((), ())), preferred_element_type=F32)


NN = ((1,), (0,))
NT = ((1,), (1,))
TN = ((0,), (0,))


def cost(flops, nbytes, trans=0):
    return pl.CostEstimate(flops=int(flops), bytes_accessed=int(nbytes), transcendentals=int(trans))


def params(axes=1):
    return pltpu.CompilerParams(dimension_semantics=("arbitrary",) * axes, vmem_limit_bytes=VMEM_LIMIT)


def means_kernel(segment, x_ref, o_ref):
    rows, tokens = o_ref.shape[0], x_ref.shape[0]
    row = lax.broadcasted_iota(jnp.int32, (rows, tokens), 0)
    col = lax.broadcasted_iota(jnp.int32, (rows, tokens), 1)
    inside = jnp.logical_and(col >= row * segment, col < (row + 1) * segment)
    pick = jnp.where(inside, 1.0, 0.0).astype(BF16)
    o_ref[...] = (dot(pick, x_ref[...], NN) / segment).astype(BF16)


def means(x, rows):
    tokens, width = x.shape
    block = min(width, 1024)
    return pl.pallas_call(
        functools.partial(means_kernel, tokens // rows),
        grid=(width // block,),
        in_specs=[pl.BlockSpec((tokens, block), lambda i: (0, i))],
        out_specs=pl.BlockSpec((rows, block), lambda i: (0, i)),
        out_shape=jax.ShapeDtypeStruct((rows, width), BF16),
        compiler_params=params(),
        cost_estimate=cost(2 * rows * tokens * width, 2 * tokens * width),
        name="means",
    )(x)


def greet(n):
    me = lax.axis_index("seq")
    barrier = pltpu.get_barrier_semaphore()
    for step in range(1, n):
        pl.semaphore_signal(
            barrier, inc=1, device_id={"seq": lax.rem(me + step, n)}, device_id_type=MESH
        )
    pl.semaphore_wait(barrier, n - 1)


def hops(n):
    ring = n // 2
    far, near = ring // 2, (ring - 1) // 2
    return ring, far, near


def copies_of(n):
    ring, far, near = hops(n)
    return 2 + 2 * (ring - 1) + 2 * (ring - 1) + 1


def gather_kernel(n, count, *refs):
    xs, outs = refs[:count], refs[count : 2 * count]
    send_sem, recv_sem, local_sem = refs[2 * count :]
    me = lax.axis_index("seq")
    ring, far, near = hops(n)
    z, x = me // 2, lax.rem(me, 2)
    partner = z * 2 + (1 - x)

    def at(steps, side):
        return lax.rem(z + steps + 2 * ring, ring) * 2 + side

    rows = xs[0].shape[0]
    half = rows // 2
    greet(n)
    local = []
    for a in range(count):
        copy = pltpu.make_async_copy(
            xs[a], outs[a].at[pl.ds(pl.multiple_of(me * rows, rows), rows)], local_sem.at[a]
        )
        copy.start()
        local.append(copy)
    used = [0] * count
    started, done = [], set()

    def send(a, part, chunk, dest, own):
        index = used[a]
        used[a] += 1
        spot = outs[a].at[pl.ds(pl.multiple_of(chunk * rows + part * half, half), half)]
        copy = pltpu.make_async_remote_copy(
            src_ref=xs[a].at[pl.ds(part * half, half)] if own else spot,
            dst_ref=spot,
            send_sem=send_sem.at[a, index],
            recv_sem=recv_sem.at[a, index],
            device_id={"seq": dest},
            device_id_type=MESH,
        )
        copy.start()
        started.append(copy)
        return len(started) - 1

    def arrived(which):
        started[which].wait_recv()
        done.add(which)

    reach = {(0, 1): far, (0, -1): near, (1, 1): near, (1, -1): far}
    live = {}
    for a in range(count):
        live[a] = send(a, 0, me, partner, True)
        for part in (1, 0):
            for way in (1, -1):
                if reach[part, way] > 0:
                    live[a, part, way, 0] = send(a, part, me, at(way, x), True)
        send(a, 1, me, partner, True)
    for a in range(count):
        arrived(live[a])
        for way in (1, -1):
            if reach[0, way] > 0:
                live[a, 0, way, 1] = send(a, 0, partner, at(way, x), False)
    for step in range(1, far + 1):
        for a in range(count):
            for part in (1, 0):
                for way in (1, -1):
                    if step > reach[part, way]:
                        continue
                    for other in range(2 - part):
                        arrived(live[a, part, way, other])
                        chunk = at(-way * step, x if other == 0 else 1 - x)
                        if step < reach[part, way]:
                            live[a, part, way, other] = send(a, part, chunk, at(way, x), False)
                        if part == 1:
                            send(a, 1, chunk, partner, False)
    for which in range(len(started)):
        if which not in done:
            arrived(which)
    for copy in started:
        copy.wait_send()
    for copy in local:
        copy.wait()


def gather(arrays, n, ident):
    count = len(arrays)
    total = copies_of(n)
    return pl.pallas_call(
        functools.partial(gather_kernel, n, count),
        in_specs=[pl.BlockSpec(memory_space=pltpu.VMEM)] * count,
        out_specs=[pl.BlockSpec(memory_space=pl.ANY)] * count,
        out_shape=[jax.ShapeDtypeStruct((n * x.shape[0], x.shape[1]), x.dtype) for x in arrays],
        scratch_shapes=[
            pltpu.SemaphoreType.DMA((count, total)),
            pltpu.SemaphoreType.DMA((count, total)),
            pltpu.SemaphoreType.DMA((count,)),
        ],
        compiler_params=pltpu.CompilerParams(collective_id=ident, has_side_effects=True),
        name="gather",
    )(*arrays)


def landmark_kernel(n, owned, lq_ref, lk_ref, k_ref, v_ref, o_ref, out_w, out_s, in_w, in_s, kern, z_ref, send_sem, recv_sem):
    me = lax.axis_index("seq")
    greet(n)

    def partial_sums(head, slot, j):
        cols = pl.ds(pl.multiple_of(head * DH, DH), DH)
        scores = dot(k_ref[:, cols], lq_ref[:, cols], NT) * SCALE
        peak = jnp.max(scores, 0, keepdims=True)
        expo = jnp.exp(scores - peak)
        out_s[slot, 2 * j : 2 * j + 1, :] = peak
        out_s[slot, 2 * j + 1 : 2 * j + 2, :] = jnp.sum(expo, 0, keepdims=True)
        out_w[slot, j * DH : (j + 1) * DH, :] = dot(v_ref[:, cols], expo.astype(BF16), TN).astype(BF16)

    def copies(step):
        dest = {"seq": lax.rem(me + step, n)}
        return [
            pltpu.make_async_remote_copy(
                src_ref=src.at[step - 1],
                dst_ref=dst.at[step - 1],
                send_sem=send_sem.at[kind, step - 1],
                recv_sem=recv_sem.at[kind, step - 1],
                device_id=dest,
                device_id_type=MESH,
            )
            for kind, (src, dst) in enumerate(((out_w, in_w), (out_s, in_s)))
        ]

    def serve(step, carry):
        owner = lax.rem(me + step, n)
        for j in range(owned):
            partial_sums(owner * owned + j, step - 1, j)
        for copy in copies(step):
            copy.start()
        return carry

    lax.fori_loop(1, n, serve, 0)
    for j in range(owned):
        partial_sums(me * owned + j, n - 1, j)

    group = 2 if owned % 2 == 0 else 1
    row = lax.broadcasted_iota(jnp.int32, (M, M), 0)
    col = lax.broadcasted_iota(jnp.int32, (M, M), 1)
    eye = row == col
    for first in range(0, owned, group):
        for g in range(group):
            cols = pl.ds(pl.multiple_of((me * owned + first + g) * DH, DH), DH)
            scores = dot(lq_ref[:, cols], lk_ref[:, cols], NT) * SCALE
            expo = jnp.exp(scores - jnp.max(scores, 1, keepdims=True))
            kernel = expo / jnp.sum(expo, 1, keepdims=True)
            row_most = jnp.max(jnp.sum(kernel, 1, keepdims=True), 0, keepdims=True)
            col_most = jnp.max(jnp.sum(kernel, 0, keepdims=True), 1, keepdims=True)
            kern[g] = kernel.astype(BF16)
            z_ref[first + g] = kernel.T / (row_most * col_most)

        def sweep(i, carry):
            low = [z_ref[first + g].astype(BF16) for g in range(group)]
            p = [dot(kern[g], low[g], NN) for g in range(group)]
            pb = [v.astype(BF16) for v in p]
            q1 = [dot(pb[g], jnp.where(eye, 7.0 - p[g], -p[g]).astype(BF16), NN) for g in range(group)]
            q2 = [dot(pb[g], jnp.where(eye, 15.0 - q1[g], -q1[g]).astype(BF16), NN) for g in range(group)]
            for g in range(group):
                z_ref[first + g] = 0.25 * dot(low[g], jnp.where(eye, 13.0 - q2[g], -q2[g]).astype(BF16), NN)
            return carry

        lax.fori_loop(0, ITERS, sweep, 0)

    def collect(step, carry):
        for copy in copies(step):
            copy.wait_recv()
        for copy in copies(step):
            copy.wait_send()
        return carry

    lax.fori_loop(1, n, collect, 0)
    for j in range(owned):
        own_peak = out_s[n - 1, 2 * j : 2 * j + 1, :]

        def highest(i, best):
            return jnp.maximum(best, in_s[i, 2 * j : 2 * j + 1, :])

        peak = lax.fori_loop(0, n - 1, highest, own_peak)
        factor = jnp.exp(own_peak - peak)
        total = factor * out_s[n - 1, 2 * j + 1 : 2 * j + 2, :]
        summed = factor * out_w[n - 1, j * DH : (j + 1) * DH, :].astype(F32)

        def add(i, carry):
            total, summed = carry
            factor = jnp.exp(in_s[i, 2 * j : 2 * j + 1, :] - peak)
            total = total + factor * in_s[i, 2 * j + 1 : 2 * j + 2, :]
            summed = summed + factor * in_w[i, j * DH : (j + 1) * DH, :].astype(F32)
            return total, summed

        total, summed = lax.fori_loop(0, n - 1, add, (total, summed))
        normed = (summed / total).astype(BF16)
        o_ref[j] = dot(z_ref[j].astype(BF16), normed, NT).astype(BF16)


def landmark_products(land_q, land_k, keys, values, n):
    owned = H // n
    group = 2 if owned % 2 == 0 else 1
    return pl.pallas_call(
        functools.partial(landmark_kernel, n, owned),
        in_specs=[pl.BlockSpec(memory_space=pltpu.VMEM)] * 4,
        out_specs=pl.BlockSpec(memory_space=pltpu.VMEM),
        out_shape=jax.ShapeDtypeStruct((owned, M, DH), BF16),
        scratch_shapes=[
            pltpu.VMEM((n, owned * DH, M), BF16),
            pltpu.VMEM((n, 2 * owned, M), F32),
            pltpu.VMEM((n - 1, owned * DH, M), BF16),
            pltpu.VMEM((n - 1, 2 * owned, M), F32),
            pltpu.VMEM((group, M, M), BF16),
            pltpu.VMEM((owned, M, M), F32),
            pltpu.SemaphoreType.DMA((2, n - 1)),
            pltpu.SemaphoreType.DMA((2, n - 1)),
        ],
        compiler_params=pltpu.CompilerParams(
            collective_id=1, has_side_effects=True, vmem_limit_bytes=VMEM_LIMIT
        ),
        name="landmark_products",
    )(land_q, land_k, keys, values)


def weights_kernel(q_ref, lk_ref, o_ref):
    scores = dot(q_ref[...], lk_ref[...], NT) * SCALE
    expo = jnp.exp(scores - jnp.max(scores, 1, keepdims=True))
    o_ref[0] = (expo / jnp.sum(expo, 1, keepdims=True)).astype(BF16)


def token_weights(queries, land_k):
    tokens = queries.shape[0]
    return pl.pallas_call(
        weights_kernel,
        grid=(H,),
        in_specs=[
            pl.BlockSpec((tokens, DH), lambda h: (0, h)),
            pl.BlockSpec((M, DH), lambda h: (0, h)),
        ],
        out_specs=pl.BlockSpec((1, tokens, M), lambda h: (h, 0, 0)),
        out_shape=jax.ShapeDtypeStruct((H, tokens, M), BF16),
        compiler_params=params(),
        cost_estimate=cost(4 * H * tokens * M * DH, 2 * H * tokens * M, H * tokens * M),
        name="weights",
    )(queries, land_k)


def attend_kernel(w_ref, p_ref, o_ref):
    o_ref[...] = dot(w_ref[0], p_ref[0], NN).astype(BF16)


def attend(weights, product):
    tokens = weights.shape[1]
    return pl.pallas_call(
        attend_kernel,
        grid=(H,),
        in_specs=[
            pl.BlockSpec((1, tokens, M), lambda h: (h, 0, 0)),
            pl.BlockSpec((1, M, DH), lambda h: (h, 0, 0)),
        ],
        out_specs=pl.BlockSpec((tokens, DH), lambda h: (0, h)),
        out_shape=jax.ShapeDtypeStruct((tokens, H * DH), BF16),
        compiler_params=params(),
        cost_estimate=cost(4 * H * tokens * M * DH, 2 * H * tokens * M),
        name="attend",
    )(weights, product)


def body(queries, keys, values):
    devices = lax.axis_size("seq")
    per_device = M // devices
    local_q = means(queries, per_device)
    local_k = means(keys, per_device)
    land_q, land_k = gather((local_q, local_k), devices, 0)
    own_product = landmark_products(land_q, land_k, keys, values, devices)
    product = lax.all_gather(own_product, "seq", axis=0, tiled=True)
    weights = token_weights(queries, land_k)
    return attend(weights, product)


def solution(mesh):
    placed = (P(("doc", "seq"), None),) * 3
    return jax.shard_map(
        body, mesh=mesh, in_specs=placed, out_specs=P(("doc", "seq"), None), check_vma=False
    )
```

time: 375 us -> 342 us (0.912)
  waiting for transfers between devices: 192 us -> 68.1 us
  Pallas kernels: 167 us -> 259 us
    pallas_call x5 -> x2, Pallas kernels: 104 us -> 196 us  [the longest x1 110 us: gather(): pl.pallas_call(functools.partial(gather_kernel, n, count), in_specs=[pl.B...]
    all_gather x2 -> x0, waiting for transfers between devices: 84.7 us -> none  [the longest x1 71.1 us: body(): land_q = lax.all_gather(local_q, 'seq', axis=0, tiled=True)]
    reduce_scatter x1 -> x0, waiting for transfers between devices: 64.1 us -> none  [body(): summed = lax.psum_scatter(partial, 'seq', scatter_dimension=0, tiled=True)]
    all_gather x1, waiting for transfers between devices: 43.4 us -> 68 us  [body(): product = lax.all_gather(own_product, 'seq', axis=0, tiled=True)]
  transfers between devices with their start and end apart: 4 -> 1, of which waited for: 4 -> 1; matrix products, arithmetic and copies ran while one was open for 0% -> 0% of each run, Pallas kernels for 36% -> 9%
where the time goes in v2:
time: 342 us; the launch traced here: 340 us
  Pallas kernels  259 us (76%)
  waiting for transfers between devices  68.1 us (20%)
  between operations  13.4 us (4%)
    pallas_call x1, Pallas kernels, gather(): pl.pallas_call(functools.partial(gather_kernel, n, count), in_specs=[pl.B...  110 us
    pallas_call x1, Pallas kernels, landmark_products(): pl.pallas_call(functools.partial(landmark_kernel, n, owned), in_specs=[pl...  85.5 us
    all_gather x1, waiting for transfers between devices, body(): product = lax.all_gather(own_product, 'seq', axis=0, tiled=True)  68 us
    pallas_call x1, Pallas kernels, token_weights(): pl.pallas_call(weights_kernel, grid=(H,), in_specs=[pl.BlockSpec((tokens,...  29.1 us
    pallas_call x1, Pallas kernels, attend(): pl.pallas_call(attend_kernel, grid=(H,), in_specs=[pl.BlockSpec((1, token...  24.6 us
    pallas_call x2, Pallas kernels, means(): pl.pallas_call(functools.partial(means_kernel, tokens // rows), grid=(wid...  8.93 us
  transfers between devices with their start and end apart: 1, of which 1 were waited for; matrix products, arithmetic and copies ran while one was open for 0% of the time, Pallas kernels for 9%

profile of v2, /device:TPU:0, one launch (start us, length us, event | category | flops | bytes accessed | tf_op | source)
XLA Modules:
  0.0 340.0 jit_solution(11260611044644655488)
XLA Ops:
  6.5 0.0 all-gather.2.cloned.1.call-start
  6.5 4.4 %means.2.refs_0_ = bf16[64,4096]{1,0:T(8,128)(2,1)} custom-call(bf16[512,4096]{1,0:T(8,128)(2,1)} %q_ref.1), custom_call_target="tpu_custom_call" | custom-call | flops 268435456 | bytes 4194304 | tf_op jit(solution)/shard_map/means/pallas_call | solution.py:50
  11.0 4.5 %means.3.refs_1_ = bf16[64,4096]{1,0:T(8,128)(2,1)} custom-call(bf16[512,4096]{1,0:T(8,128)(2,1)} %k_ref.1), custom_call_target="tpu_custom_call" | custom-call | flops 268435456 | bytes 4194304 | tf_op jit(solution)/shard_map/means/pallas_call | solution.py:50
  15.5 110.3 %gather.1 = (bf16[512,4096]{1,0:T(8,128)(2,1)}, bf16[512,4096]{1,0:T(8,128)(2,1)}) custom-call(bf16[64,4096]{1,0:T(8,128)(2,1)} %means.2.refs_0_, bf16[64,4096]{1,0:T(8,128)(2,1)} %means.3.refs_1_), custom_call_target="tpu_custom_call" | custom-call | tf_op jit(solution)/shard_map/gather/pallas_call | solution.py:166
  125.8 85.5 %landmark_products.1 = bf16[4,512,128]{2,1,0:T(8,128)(2,1)} custom-call(bf16[512,4096]{1,0:T(8,128)(2,1)} %get-tuple-element.8.lq_ref, bf16[512,4096]{1,0:T(8,128)(2,1)} %get-tuple-element.7.lk_ref, bf16[512,4096]{1,0:T(8,128)(2,1)} %k_ref.1, bf16[512,4096]{1,0:T(8,128)(2,1)} %v_ref.1), custom_call_target="tpu_custom_call" | custom-call | tf_op jit(solution)/shard_map/landmark_products/pallas_call | solution.py:281
  211.3 0.0 all-gather.2.cloned.1.call-update
  211.4 29.1 %weights.1.w_ref = bf16[32,512,512]{2,1,0:T(8,128)(2,1)} custom-call(bf16[512,4096]{1,0:T(8,128)(2,1)} %q_ref.1, bf16[512,4096]{1,0:T(8,128)(2,1)} %get-tuple-element.7.lk_ref), custom_call_target="tpu_custom_call" | custom-call | flops 4294967296 | bytes 16777216 | tf_op jit(solution)/shard_map/weights/pallas_call | solution.py:311
  240.5 68.0 %all-gather.2.cloned.1.call-done.p_ref = bf16[32,512,128]{2,1,0:T(8,128)(2,1)} async-done(((bf16[4,512,128]{2,1,0:T(8,128)(2,1)}), bf16[32,512,128]{2,1,0:T(8,128)(2,1)}) %all-gather.2.cloned.1.call-update) | async-done | bytes 4194320 | tf_op jit(solution)/shard_map/all_gather | solution.py:354
  308.5 24.6 %attend.1 = bf16[512,4096]{1,0:T(8,128)(2,1)} custom-call(bf16[32,512,512]{2,1,0:T(8,128)(2,1)} %weights.1.w_ref, bf16[32,512,128]{2,1,0:T(8,128)(2,1)} %all-gather.2.cloned.1.call-done.p_ref), custom_call_target="tpu_custom_call" | custom-call | flops 4294967296 | bytes 16777216 | tf_op jit(solution)/shard_map/attend/pallas_call | solution.py:332
Async XLA Ops:
  6.5 302.0 %all-gather.2.cloned.1.call-start = ((), (), s32[]{:S(2)}) async-start(), calls=%async_computation | async-start | bytes 4718592 | tf_op jit(solution)/shard_map/all_gather | solution.py:354
Sparse Core Ops, SparseCore 0:
  211.5 97.0 all-gather.1

commit v3 on v2

--- a/solution.py
+++ b/solution.py
@@ -80,9 +80,8 @@
     return 2 + 2 * (ring - 1) + 2 * (ring - 1) + 1
 
 
-def gather_kernel(n, count, *refs):
-    xs, outs = refs[:count], refs[count : 2 * count]
-    send_sem, recv_sem, local_sem = refs[2 * count :]
+def gather_stages(n, xs, outs, send_sem, recv_sem, local_sem):
+    count = len(xs)
     me = lax.axis_index("seq")
     ring, far, near = hops(n)
     z, x = me // 2, lax.rem(me, 2)
@@ -92,7 +91,8 @@
         return lax.rem(z + steps + 2 * ring, ring) * 2 + side
 
     rows = xs[0].shape[0]
-    half = rows // 2
+    first = max(8, rows // 64 * 8)
+    spans = ((0, first), (first, rows - first))
     greet(n)
     local = []
     for a in range(count):
@@ -107,9 +107,10 @@
     def send(a, part, chunk, dest, own):
         index = used[a]
         used[a] += 1
-        spot = outs[a].at[pl.ds(pl.multiple_of(chunk * rows + part * half, half), half)]
+        low, size = spans[part]
+        spot = outs[a].at[pl.ds(pl.multiple_of(chunk * rows + low, 8), size)]
         copy = pltpu.make_async_remote_copy(
-            src_ref=xs[a].at[pl.ds(part * half, half)] if own else spot,
+            src_ref=xs[a].at[pl.ds(low, size)] if own else spot,
             dst_ref=spot,
             send_sem=send_sem.at[a, index],
             recv_sem=recv_sem.at[a, index],
@@ -133,12 +134,14 @@
                 if reach[part, way] > 0:
                     live[a, part, way, 0] = send(a, part, me, at(way, x), True)
         send(a, 1, me, partner, True)
+    yield
     for a in range(count):
         arrived(live[a])
         for way in (1, -1):
             if reach[0, way] > 0:
                 live[a, 0, way, 1] = send(a, 0, partner, at(way, x), False)
     for step in range(1, far + 1):
+        yield
         for a in range(count):
             for part in (1, 0):
                 for way in (1, -1):
@@ -151,6 +154,7 @@
                             live[a, part, way, other] = send(a, part, chunk, at(way, x), False)
                         if part == 1:
                             send(a, 1, chunk, partner, False)
+    yield
     for which in range(len(started)):
         if which not in done:
             arrived(which)
@@ -158,6 +162,11 @@
         copy.wait_send()
     for copy in local:
         copy.wait()
+
+
+def gather_kernel(n, count, *refs):
+    for _ in gather_stages(n, refs[:count], refs[count : 2 * count], *refs[2 * count :]):
+        pass
 
 
 def gather(arrays, n, ident):
@@ -300,48 +309,50 @@
     )(land_q, land_k, keys, values)
 
 
-def weights_kernel(q_ref, lk_ref, o_ref):
-    scores = dot(q_ref[...], lk_ref[...], NT) * SCALE
-    expo = jnp.exp(scores - jnp.max(scores, 1, keepdims=True))
-    o_ref[0] = (expo / jnp.sum(expo, 1, keepdims=True)).astype(BF16)
-
-
-def token_weights(queries, land_k):
-    tokens = queries.shape[0]
+def final_kernel(n, own_ref, q_ref, lk_ref, o_ref, held, weights, send_sem, recv_sem, local_sem):
+    def weigh(head, carry):
+        cols = pl.ds(pl.multiple_of(head * DH, DH), DH)
+        scores = dot(q_ref[:, cols], lk_ref[:, cols], NT) * SCALE
+        expo = jnp.exp(scores - jnp.max(scores, 1, keepdims=True))
+        weights[head] = (expo / jnp.sum(expo, 1, keepdims=True)).astype(BF16)
+        return carry
+
+    pieces = hops(n)[1] + 2
+    at = 0
+    for piece, _ in enumerate(gather_stages(n, [own_ref], [held], send_sem, recv_sem, local_sem)):
+        until = H * (piece + 1) // pieces
+        lax.fori_loop(at, until, weigh, 0)
+        at = until
+
+    def attend(head, carry):
+        cols = pl.ds(pl.multiple_of(head * DH, DH), DH)
+        rows = pl.ds(pl.multiple_of(head * M, M), M)
+        o_ref[:, cols] = dot(weights[head], held[rows, :], NN).astype(BF16)
+        return carry
+
+    lax.fori_loop(0, H, attend, 0)
+
+
+def final(own_product, queries, land_k, n):
+    tokens, width = queries.shape
+    total = copies_of(n)
     return pl.pallas_call(
-        weights_kernel,
-        grid=(H,),
-        in_specs=[
-            pl.BlockSpec((tokens, DH), lambda h: (0, h)),
-            pl.BlockSpec((M, DH), lambda h: (0, h)),
+        functools.partial(final_kernel, n),
+        in_specs=[pl.BlockSpec(memory_space=pltpu.VMEM)] * 3,
+        out_specs=pl.BlockSpec(memory_space=pltpu.VMEM),
+        out_shape=jax.ShapeDtypeStruct((tokens, width), BF16),
+        scratch_shapes=[
+            pltpu.VMEM((H * M, DH), BF16),
+            pltpu.VMEM((H, tokens, M), BF16),
+            pltpu.SemaphoreType.DMA((1, total)),
+            pltpu.SemaphoreType.DMA((1, total)),
+            pltpu.SemaphoreType.DMA((1,)),
         ],
-        out_specs=pl.BlockSpec((1, tokens, M), lambda h: (h, 0, 0)),
-        out_shape=jax.ShapeDtypeStruct((H, tokens, M), BF16),
-        compiler_params=params(),
-        cost_estimate=cost(4 * H * tokens * M * DH, 2 * H * tokens * M, H * tokens * M),
-        name="weights",
-    )(queries, land_k)
-
-
-def attend_kernel(w_ref, p_ref, o_ref):
-    o_ref[...] = dot(w_ref[0], p_ref[0], NN).astype(BF16)
-
-
-def attend(weights, product):
-    tokens = weights.shape[1]
-    return pl.pallas_call(
-        attend_kernel,
-        grid=(H,),
-        in_specs=[
-            pl.BlockSpec((1, tokens, M), lambda h: (h, 0, 0)),
-            pl.BlockSpec((1, M, DH), lambda h: (h, 0, 0)),
-        ],
-        out_specs=pl.BlockSpec((tokens, DH), lambda h: (0, h)),
-        out_shape=jax.ShapeDtypeStruct((tokens, H * DH), BF16),
-        compiler_params=params(),
-        cost_estimate=cost(4 * H * tokens * M * DH, 2 * H * tokens * M),
-        name="attend",
-    )(weights, product)
+        compiler_params=pltpu.CompilerParams(
+            collective_id=2, has_side_effects=True, vmem_limit_bytes=VMEM_LIMIT
+        ),
+        name="final",
+    )(own_product, queries, land_k)
 
 
 def body(queries, keys, values):
@@ -351,9 +362,7 @@
     local_k = means(keys, per_device)
     land_q, land_k = gather((local_q, local_k), devices, 0)
     own_product = landmark_products(land_q, land_k, keys, values, devices)
-    product = lax.all_gather(own_product, "seq", axis=0, tiled=True)
-    weights = token_weights(queries, land_k)
-    return attend(weights, product)
+    return final(own_product.reshape(-1, DH), queries, land_k, devices)
 
 
 def solution(mesh):

time: 342 us -> 288 us (0.84)
  waiting for transfers between devices: 68.1 us -> 0 us
  Pallas kernels: 259 us -> 283 us
  between operations: 13.4 us -> 0.03 us
  local copies, waits for them, and re-layouts: 0 us -> 4.7 us
    all_gather x1 -> x0, waiting for transfers between devices: 68 us -> none  [body(): product = lax.all_gather(own_product, 'seq', axis=0, tiled=True)]
    pallas_call x2 -> x1, Pallas kernels: 53.7 us -> 90 us  [final(): pl.pallas_call(functools.partial(final_kernel, n), in_specs=[pl.BlockSpec...]
    pallas_call x1, Pallas kernels: 110 us -> 98.4 us  [gather(): pl.pallas_call(functools.partial(gather_kernel, n, count), in_specs=[pl.B...]
    unnamed x0 -> x1, local copies, waits for them, and re-layouts: none -> 4.7 us
  transfers between devices with their start and end apart: 1 -> 0, of which waited for: 1 -> 0; matrix products, arithmetic and copies ran while one was open for 0% -> 0% of each run, Pallas kernels for 9% -> 0%
where the time goes in v3:
time: 288 us
  Pallas kernels  283 us (98%)
  local copies, waits for them, and re-layouts  4.7 us (2%)
    pallas_call x1, Pallas kernels, gather(): pl.pallas_call(functools.partial(gather_kernel, n, count), in_specs=[pl.B...  98.4 us
    pallas_call x1, Pallas kernels, final(): pl.pallas_call(functools.partial(final_kernel, n), in_specs=[pl.BlockSpec...  90 us
    pallas_call x1, Pallas kernels, landmark_products(): pl.pallas_call(functools.partial(landmark_kernel, n, owned), in_specs=[pl...  85.9 us
    pallas_call x2, Pallas kernels, means(): pl.pallas_call(functools.partial(means_kernel, tokens // rows), grid=(wid...  8.88 us

profile of v3, /device:TPU:0, one launch (start us, length us, event | category | flops | bytes accessed | tf_op | source)
XLA Modules:
  0.0 287.9 jit_solution(7952644284971654430)
XLA Ops:
  0.0 4.4 %means.2.refs_0_ = bf16[64,4096]{1,0:T(8,128)(2,1)} custom-call(bf16[512,4096]{1,0:T(8,128)(2,1)} %q_ref.1), custom_call_target="tpu_custom_call" | custom-call | flops 268435456 | bytes 4194304 | tf_op jit(solution)/shard_map/means/pallas_call | solution.py:50
  4.4 4.4 %means.3.refs_1_ = bf16[64,4096]{1,0:T(8,128)(2,1)} custom-call(bf16[512,4096]{1,0:T(8,128)(2,1)} %k_ref.1), custom_call_target="tpu_custom_call" | custom-call | flops 268435456 | bytes 4194304 | tf_op jit(solution)/shard_map/means/pallas_call | solution.py:50
  8.9 98.4 %gather.1 = (bf16[512,4096]{1,0:T(8,128)(2,1)}, bf16[512,4096]{1,0:T(8,128)(2,1)}) custom-call(bf16[64,4096]{1,0:T(8,128)(2,1)} %means.2.refs_0_, bf16[64,4096]{1,0:T(8,128)(2,1)} %means.3.refs_1_), custom_call_target="tpu_custom_call" | custom-call | tf_op jit(solution)/shard_map/gather/pallas_call | solution.py:175
  107.3 85.9 %landmark_products.1 = bf16[4,512,128]{2,1,0:T(8,128)(2,1)} custom-call(bf16[512,4096]{1,0:T(8,128)(2,1)} %get-tuple-element.7.lq_ref, bf16[512,4096]{1,0:T(8,128)(2,1)} %get-tuple-element.8.lk_ref, bf16[512,4096]{1,0:T(8,128)(2,1)} %k_ref.1, bf16[512,4096]{1,0:T(8,128)(2,1)} %v_ref.1), custom_call_target="tpu_custom_call" | custom-call | tf_op jit(solution)/shard_map/landmark_products/pallas_call | solution.py:290
  193.2 90.0 %final.1 = bf16[512,4096]{1,0:T(8,128)(2,1)} custom-call(bf16[2048,128]{1,0:T(8,128)(2,1)} %bitcast.1, bf16[512,4096]{1,0:T(8,128)(2,1)} %q_ref.1, bf16[512,4096]{1,0:T(8,128)(2,1)} %get-tuple-element.8.lk_ref), custom_call_target="tpu_custom_call" | custom-call | tf_op jit(solution)/shard_map/final/pallas_call | solution.py:339
  283.2 4.7 %copy.5 = bf16[512,4096]{1,0:T(8,128)(2,1)} copy(bf16[512,4096]{1,0:T(8,128)(2,1)} %final.1) | data formatting | bytes 8388608

commit v4 on v3

--- a/solution.py
+++ b/solution.py
@@ -187,9 +187,11 @@
     )(*arrays)
 
 
-def landmark_kernel(n, owned, lq_ref, lk_ref, k_ref, v_ref, o_ref, out_w, out_s, in_w, in_s, kern, z_ref, send_sem, recv_sem):
+def landmark_kernel(
+    n, owned, lq_ref, x_ref, k_ref, v_ref, o_ref, lk_ref, out_w, out_s, in_w, in_s, kern, z_ref, own_k,
+    send_sem, recv_sem, ring_send, ring_recv, local_sem, own_sem,
+):
     me = lax.axis_index("seq")
-    greet(n)
 
     def partial_sums(head, slot, j):
         cols = pl.ds(pl.multiple_of(head * DH, DH), DH)
@@ -214,7 +216,8 @@
             for kind, (src, dst) in enumerate(((out_w, in_w), (out_s, in_s)))
         ]
 
-    def serve(step, carry):
+    def serve(turn, carry):
+        step = n // 2 + (turn + 1) // 2 * (1 - 2 * lax.rem(turn, 2))
         owner = lax.rem(me + step, n)
         for j in range(owned):
             partial_sums(owner * owned + j, step - 1, j)
@@ -222,9 +225,19 @@
             copy.start()
         return carry
 
-    lax.fori_loop(1, n, serve, 0)
-    for j in range(owned):
-        partial_sums(me * owned + j, n - 1, j)
+    pieces = hops(n)[1] + 2
+    at = 0
+    for piece, _ in enumerate(gather_stages(n, [x_ref], [lk_ref], ring_send, ring_recv, local_sem)):
+        until = (n - 1) * (piece + 1) // pieces
+        lax.fori_loop(at, until, serve, 0)
+        at = until
+        if piece == pieces - 1:
+            for j in range(owned):
+                partial_sums(me * owned + j, n - 1, j)
+    own_cols = pl.ds(pl.multiple_of(me * owned * DH, DH), owned * DH)
+    fetch = pltpu.make_async_copy(lk_ref.at[:, own_cols], own_k, own_sem)
+    fetch.start()
+    fetch.wait()
 
     group = 2 if owned % 2 == 0 else 1
     row = lax.broadcasted_iota(jnp.int32, (M, M), 0)
@@ -233,7 +246,7 @@
     for first in range(0, owned, group):
         for g in range(group):
             cols = pl.ds(pl.multiple_of((me * owned + first + g) * DH, DH), DH)
-            scores = dot(lq_ref[:, cols], lk_ref[:, cols], NT) * SCALE
+            scores = dot(lq_ref[:, cols], own_k[:, (first + g) * DH : (first + g + 1) * DH], NT) * SCALE
             expo = jnp.exp(scores - jnp.max(scores, 1, keepdims=True))
             kernel = expo / jnp.sum(expo, 1, keepdims=True)
             row_most = jnp.max(jnp.sum(kernel, 1, keepdims=True), 0, keepdims=True)
@@ -284,14 +297,17 @@
         o_ref[j] = dot(z_ref[j].astype(BF16), normed, NT).astype(BF16)
 
 
-def landmark_products(land_q, land_k, keys, values, n):
+def landmark_products(land_q, local_k, keys, values, n):
     owned = H // n
     group = 2 if owned % 2 == 0 else 1
     return pl.pallas_call(
         functools.partial(landmark_kernel, n, owned),
         in_specs=[pl.BlockSpec(memory_space=pltpu.VMEM)] * 4,
-        out_specs=pl.BlockSpec(memory_space=pltpu.VMEM),
-        out_shape=jax.ShapeDtypeStruct((owned, M, DH), BF16),
+        out_specs=[pl.BlockSpec(memory_space=pltpu.VMEM), pl.BlockSpec(memory_space=pl.ANY)],
+        out_shape=[
+            jax.ShapeDtypeStruct((owned, M, DH), BF16),
+            jax.ShapeDtypeStruct((n * local_k.shape[0], local_k.shape[1]), BF16),
+        ],
         scratch_shapes=[
             pltpu.VMEM((n, owned * DH, M), BF16),
             pltpu.VMEM((n, 2 * owned, M), F32),
@@ -299,14 +315,19 @@
             pltpu.VMEM((n - 1, 2 * owned, M), F32),
             pltpu.VMEM((group, M, M), BF16),
             pltpu.VMEM((owned, M, M), F32),
+            pltpu.VMEM((M, owned * DH), BF16),
             pltpu.SemaphoreType.DMA((2, n - 1)),
             pltpu.SemaphoreType.DMA((2, n - 1)),
+            pltpu.SemaphoreType.DMA((1, copies_of(n))),
+            pltpu.SemaphoreType.DMA((1, copies_of(n))),
+            pltpu.SemaphoreType.DMA((1,)),
+            pltpu.SemaphoreType.DMA,
         ],
         compiler_params=pltpu.CompilerParams(
             collective_id=1, has_side_effects=True, vmem_limit_bytes=VMEM_LIMIT
         ),
         name="landmark_products",
-    )(land_q, land_k, keys, values)
+    )(land_q, local_k, keys, values)
 
 
 def final_kernel(n, own_ref, q_ref, lk_ref, o_ref, held, weights, send_sem, recv_sem, local_sem):
@@ -360,8 +381,8 @@
     per_device = M // devices
     local_q = means(queries, per_device)
     local_k = means(keys, per_device)
-    land_q, land_k = gather((local_q, local_k), devices, 0)
-    own_product = landmark_products(land_q, land_k, keys, values, devices)
+    (land_q,) = gather((local_q,), devices, 0)
+    own_product, land_k = landmark_products(land_q, local_k, keys, values, devices)
     return final(own_product.reshape(-1, DH), queries, land_k, devices)
 
 

time: 288 us -> 309 us (1.073)
  Pallas kernels: 283 us -> 304 us
    pallas_call x1, Pallas kernels: 85.9 us -> 131 us  [landmark_products(): pl.pallas_call(functools.partial(landmark_kernel, n, owned), in_specs=[pl...]
    pallas_call x1, Pallas kernels: 98.4 us -> 56.1 us  [gather(): pl.pallas_call(functools.partial(gather_kernel, n, count), in_specs=[pl.B...]
    pallas_call x1, Pallas kernels: 90 us -> 108 us  [final(): pl.pallas_call(functools.partial(final_kernel, n), in_specs=[pl.BlockSpec...]
where the time goes in v4:
time: 309 us; the launch traced here: 308 us
  Pallas kernels  304 us (98%)
  local copies, waits for them, and re-layouts  4.7 us (2%)
    pallas_call x1, Pallas kernels, landmark_products(): pl.pallas_call(functools.partial(landmark_kernel, n, owned), in_specs=[pl...  131 us
    pallas_call x1, Pallas kernels, final(): pl.pallas_call(functools.partial(final_kernel, n), in_specs=[pl.BlockSpec...  108 us
    pallas_call x1, Pallas kernels, gather(): pl.pallas_call(functools.partial(gather_kernel, n, count), in_specs=[pl.B...  56.1 us
    pallas_call x2, Pallas kernels, means(): pl.pallas_call(functools.partial(means_kernel, tokens // rows), grid=(wid...  8.89 us

profile of v4, /device:TPU:0, one launch (start us, length us, event | category | flops | bytes accessed | tf_op | source)
XLA Modules:
  0.0 308.4 jit_solution(8267874928993254533)
XLA Ops:
  0.0 4.4 %means.2.refs_0_ = bf16[64,4096]{1,0:T(8,128)(2,1)} custom-call(bf16[512,4096]{1,0:T(8,128)(2,1)} %q_ref.1), custom_call_target="tpu_custom_call" | custom-call | flops 268435456 | bytes 4194304 | tf_op jit(solution)/shard_map/means/pallas_call | solution.py:50
  4.4 4.4 %means.3.x_ref = bf16[64,4096]{1,0:T(8,128)(2,1)} custom-call(bf16[512,4096]{1,0:T(8,128)(2,1)} %k_ref.1), custom_call_target="tpu_custom_call" | custom-call | flops 268435456 | bytes 4194304 | tf_op jit(solution)/shard_map/means/pallas_call | solution.py:50
  8.9 56.1 %gather.1.lq_ref = bf16[512,4096]{1,0:T(8,128)(2,1)} custom-call(bf16[64,4096]{1,0:T(8,128)(2,1)} %means.2.refs_0_), custom_call_target="tpu_custom_call" | custom-call | tf_op jit(solution)/shard_map/gather/pallas_call | solution.py:175
  65.0 130.9 %landmark_products.1 = (bf16[4,512,128]{2,1,0:T(8,128)(2,1)}, bf16[512,4096]{1,0:T(8,128)(2,1)}) custom-call(bf16[512,4096]{1,0:T(8,128)(2,1)} %gather.1.lq_ref, bf16[64,4096]{1,0:T(8,128)(2,1)} %means.3.x_ref, bf16[512,4096]{1,0:T(8,128)(2,1)} %k_ref.1, bf16[512,4096]{1,0:T(8,128)(2,1)} %v_ref.1), custom_call_target="tpu_custom_call" | custom-call | tf_op jit(solution)/shard_map/landmark_products/pallas_call | solution.py:303
  195.9 107.9 %final.1 = bf16[512,4096]{1,0:T(8,128)(2,1)} custom-call(bf16[2048,128]{1,0:T(8,128)(2,1)} %bitcast.1, bf16[512,4096]{1,0:T(8,128)(2,1)} %q_ref.1, bf16[512,4096]{1,0:T(8,128)(2,1)} %get-tuple-element.8.lk_ref), custom_call_target="tpu_custom_call" | custom-call | tf_op jit(solution)/shard_map/final/pallas_call | solution.py:360
  303.7 4.7 %copy.5 = bf16[512,4096]{1,0:T(8,128)(2,1)} copy(bf16[512,4096]{1,0:T(8,128)(2,1)} %final.1) | data formatting | bytes 8388608
